TPU v7x, 32 devices: a whole 2x2x4 slice. The times are simulated.
32 devices in a mesh: blk: 16 (over z, y, core), uly: 2 (over x).
Axes of the slice: x: 2, y: 2, z: 4, core: 2. Of those that a mesh axis runs over, the one named last changes fastest.
Arguments:
- tokens: bfloat16 [4096, 5120], P(('blk', 'uly')), may hold values from -6 to 6
- query_base: bfloat16 [4096, 5120], P(('blk', 'uly')), may hold values from -9 to 9
- key_base: bfloat16 [4096, 5120], P(('blk', 'uly')), may hold values from -9 to 9
- value_base: bfloat16 [4096, 5120], P(('blk', 'uly')), may hold values from -6 to 6
- out_grad: bfloat16 [4096, 5120], P(('blk', 'uly')), may hold values from -0.059814453 to 0.059814453
- down_q: bfloat16 [5120, 64], replicated, may hold values from -0.078125 to 0.078125
- up_q: bfloat16 [64, 5120], replicated, may hold values from -0.75 to 0.75
- down_v: bfloat16 [5120, 64], replicated, may hold values from -0.078125 to 0.078125
- up_v: bfloat16 [64, 5120], replicated, may hold values from -0.75 to 0.75
Outputs:
- attended: bfloat16 [4096, 5120], P(('blk', 'uly'))
- grad_down_q: bfloat16 [5120, 64], replicated
- grad_up_q: bfloat16 [64, 5120], P(None, 'uly')
- grad_down_v: bfloat16 [5120, 64], replicated
- grad_up_v: bfloat16 [64, 5120], P(None, 'uly')
All inputs are finite; a program needn't handle non-finite values.
Results may differ from a plain program's by a relative error of at most 0.025.
Values may be sent and summed in bfloat16 or wider, within the bound.
A program may use at most 128 MiB of HBM per device.

v0:
```python
import jax
import jax.numpy as jnp
from jax import lax
from jax.sharding import PartitionSpec as P

HEAD = 128


def passed_along(block, axis, distance):
    devices = range(lax.axis_size(axis))
    route = [(i - distance, i) for i in devices if i - distance in devices]
    return lax.ppermute(block, axis, route)


def inner(left, right):
    return lax.dot_general(
        left, right, (((0,), (0,)), ((), ())), preferred_element_type=jnp.float32
    )


def head_pass(query, keys, values, upstream, usable, scale):
    scores = jnp.dot(query, keys.T, preferred_element_type=jnp.float32) * scale
    scores = jnp.where(usable[None, :], scores, -jnp.inf)
    top = jnp.max(scores, axis=1, keepdims=True)
    total = jnp.sum(jnp.exp(scores - top), axis=1, keepdims=True)
    probs = jnp.exp(scores - top - jnp.log(total)).astype(jnp.bfloat16)
    attended = jnp.dot(probs, values, preferred_element_type=jnp.float32).astype(jnp.bfloat16)
    delta = jnp.sum(
        upstream.astype(jnp.float32) * attended.astype(jnp.float32), axis=1, keepdims=True
    )
    prob_grad = jnp.dot(upstream, values.T, preferred_element_type=jnp.float32)
    score_grad = (probs.astype(jnp.float32) * (prob_grad - delta)).astype(jnp.bfloat16)
    query_grad = (jnp.dot(score_grad, keys, preferred_element_type=jnp.float32) * scale).astype(
        jnp.bfloat16
    )
    value_terms = jnp.dot(probs.T, upstream, preferred_element_type=jnp.float32)
    return (attended, query_grad, value_terms)


def per_device(tokens, query_base, key_base, value_base, out_grad, down_q, up_q, down_v, up_v):
    low_q = jnp.dot(tokens, down_q, preferred_element_type=jnp.float32).astype(jnp.bfloat16)
    low_v = jnp.dot(tokens, down_v, preferred_element_type=jnp.float32).astype(jnp.bfloat16)
    query = (
        query_base.astype(jnp.float32) + jnp.dot(low_q, up_q, preferred_element_type=jnp.float32)
    ).astype(jnp.bfloat16)
    value = (
        value_base.astype(jnp.float32) + jnp.dot(low_v, up_v, preferred_element_type=jnp.float32)
    ).astype(jnp.bfloat16)
    query_h, keys_h, values_h, upstream_h = (
        lax.all_to_all(query, "uly", split_axis=1, concat_axis=0, tiled=True),
        lax.all_to_all(key_base, "uly", split_axis=1, concat_axis=0, tiled=True),
        lax.all_to_all(value, "uly", split_axis=1, concat_axis=0, tiled=True),
        lax.all_to_all(out_grad, "uly", split_axis=1, concat_axis=0, tiled=True),
    )
    rows = query_h.shape[0]
    width = query_h.shape[1]
    heads_here = width // HEAD
    scale = HEAD ** (-0.5)
    earlier = passed_along(jnp.stack([keys_h, values_h]), "blk", 1)
    keys_all = jnp.concatenate([earlier[0], keys_h], 0)
    values_all = jnp.concatenate([earlier[1], values_h], 0)
    column = jnp.arange(2 * rows)
    usable = jnp.logical_or(column >= rows, lax.axis_index("blk") > 0)

    def per_head(index, carry):
        attended, query_grad, own_terms, prior_terms = carry
        start = index * HEAD
        result = head_pass(
            lax.dynamic_slice_in_dim(query_h, start, HEAD, 1),
            lax.dynamic_slice_in_dim(keys_all, start, HEAD, 1),
            lax.dynamic_slice_in_dim(values_all, start, HEAD, 1),
            lax.dynamic_slice_in_dim(upstream_h, start, HEAD, 1),
            usable,
            scale,
        )
        attended = lax.dynamic_update_slice_in_dim(attended, result[0], start, 1)
        query_grad = lax.dynamic_update_slice_in_dim(query_grad, result[1], start, 1)
        prior_terms = lax.dynamic_update_slice_in_dim(prior_terms, result[2][:rows], start, 1)
        own_terms = lax.dynamic_update_slice_in_dim(own_terms, result[2][rows:], start, 1)
        return (attended, query_grad, own_terms, prior_terms)

    empty_half = jnp.zeros((rows, width), jnp.bfloat16)
    empty_full = jnp.zeros((rows, width), jnp.float32)
    attended_h, query_grad_h, own_terms, prior_terms = lax.fori_loop(
        0, heads_here, per_head, (empty_half, empty_half, empty_full, empty_full)
    )
    returned = passed_along(prior_terms, "blk", -1)
    value_grad_h = (own_terms + returned).astype(jnp.bfloat16)
    rank = down_q.shape[1]
    first_col = lax.axis_index("uly") * width
    attended = lax.all_to_all(attended_h, "uly", split_axis=0, concat_axis=1, tiled=True)
    block_lows = lax.all_gather(jnp.concatenate([low_q, low_v], 1), "uly", axis=0, tiled=True)
    cols_q = lax.dynamic_slice_in_dim(up_q, first_col, width, 1)
    cols_v = lax.dynamic_slice_in_dim(up_v, first_col, width, 1)
    partial_rank = jnp.concatenate(
        [
            jnp.dot(query_grad_h, cols_q.T, preferred_element_type=jnp.float32),
            jnp.dot(value_grad_h, cols_v.T, preferred_element_type=jnp.float32),
        ],
        1,
    )
    lowrank = lax.psum_scatter(partial_rank, "uly", scatter_dimension=0, tiled=True).astype(
        jnp.bfloat16
    )
    down_total = lax.psum(inner(tokens, lowrank), ("blk", "uly"))
    up_q_terms = inner(block_lows[:, :rank], query_grad_h)
    up_v_terms = inner(block_lows[:, rank:], value_grad_h)
    up_q_part, up_v_part = (
        lax.psum(up_q_terms.astype(jnp.bfloat16), "blk").astype(jnp.float32),
        lax.psum(up_v_terms.astype(jnp.bfloat16), "blk").astype(jnp.float32),
    )
    return (
        attended,
        down_total[:, :rank].astype(jnp.bfloat16),
        up_q_part.astype(jnp.bfloat16),
        down_total[:, rank:].astype(jnp.bfloat16),
        up_v_part.astype(jnp.bfloat16),
    )


def solution(mesh):
    return jax.shard_map(
        per_device,
        mesh=mesh,
        in_specs=(
            P(("blk", "uly"), None),
            P(("blk", "uly"), None),
            P(("blk", "uly"), None),
            P(("blk", "uly"), None),
            P(("blk", "uly"), None),
            P(),
            P(),
            P(),
            P(),
        ),
        out_specs=(P(("blk", "uly"), None), P(), P(None, "uly"), P(), P(None, "uly")),
        check_vma=False,
    )
```

profile of v0, /device:TPU:0, one launch (start us, length us, event | category | flops | bytes accessed | tf_op | source)
XLA Modules:
  0.0 393.2 jit_solution(3088520763562678787)
XLA Ops:
  8.0 1.3 copy-done
  9.3 1.7 convolution_convert_fusion.3
  12.7 4.2 %all-to-all-start.2 = ((bf16[128,2,2560]{2,0,1:T(8,128)(2,1)}), bf16[128,2,2560]{2,0,1:T(8,128)(2,1)S(1)}, u32[]{:S(2)}, u32[]{:S(2)}) async-start(bf16[128,2,2560]{2,0,1:T(8,128)(2,1)} %bitcast.73), calls=%async_computation.2 | async-start | bytes 2621440 | tf_op jit(solution)/shard_map/all_to_all | solution.py:52
  16.9 2.5 copy.47
  19.4 14.8 %all-to-all-done.2 = bf16[128,2,2560]{2,0,1:T(8,128)(2,1)S(1)} async-done(((bf16[128,2,2560]{2,0,1:T(8,128)(2,1)}), bf16[128,2,2560]{2,0,1:T(8,128)(2,1)S(1)}, u32[]{:S(2)}, u32[]{:S(2)}) %all-to-all-start.2) | async-done | bytes 1310752 | tf_op jit(solution)/shard_map/all_to_all | solution.py:52
  34.2 19.7 %all_to_all.95 = bf16[128,2,2560]{2,0,1:T(8,128)(2,1)S(1)} all-to-all(bf16[128,2,2560]{2,0,1:T(8,128)(2,1)} %bitcast.74), channel_id=1, replica_groups=mesh['blk'=16,'uly'=2] {'uly'}, dimensions={1} | all-to-all | bytes 2621440 | tf_op jit(solution)/shard_map/all_to_all | solution.py:51
  53.9 1.9 pad_maximum_fusion
  55.8 2.8 collective-permute-start
  58.6 2.5 copy.30
  61.1 4.6 %all-to-all-start.3 = ((bf16[128,2,2560]{0,2,1:T(8,128)(2,1)}), bf16[128,2,2560]{0,2,1:T(8,128)(2,1)}, u32[]{:S(2)}, u32[]{:S(2)}) async-start(bf16[128,2,2560]{0,2,1:T(8,128)(2,1)} %bitcast.71), calls=%async_computation.3 | async-start | bytes 2621440 | tf_op jit(solution)/shard_map/all_to_all | solution.py:53
  69.0 14.5 %all-to-all-done.3 = bf16[128,2,2560]{0,2,1:T(8,128)(2,1)} async-done(((bf16[128,2,2560]{0,2,1:T(8,128)(2,1)}), bf16[128,2,2560]{0,2,1:T(8,128)(2,1)}, u32[]{:S(2)}, u32[]{:S(2)}) %all-to-all-start.3) | async-done | bytes 1310752 | tf_op jit(solution)/shard_map/all_to_all | solution.py:53
  83.4 4.5 %all-to-all-start = ((bf16[128,2,2560]{2,0,1:T(8,128)(2,1)}), bf16[128,2,2560]{2,0,1:T(8,128)(2,1)}, u32[]{:S(2)}, u32[]{:S(2)}) async-start(bf16[128,2,2560]{2,0,1:T(8,128)(2,1)} %bitcast.70), calls=%async_computation | async-start | bytes 2621440 | tf_op jit(solution)/shard_map/all_to_all | solution.py:50
  88.0 2.5 copy.31
  90.4 2.0 slice_bitcast_fusion
  92.5 2.5 pad_maximum_fusion.1
  95.1 9.7 %all-to-all-done = bf16[128,2,2560]{2,0,1:T(8,128)(2,1)} async-done(((bf16[128,2,2560]{2,0,1:T(8,128)(2,1)}), bf16[128,2,2560]{2,0,1:T(8,128)(2,1)}, u32[]{:S(2)}, u32[]{:S(2)}) %all-to-all-start) | async-done | bytes 1310752 | tf_op jit(solution)/shard_map/all_to_all | solution.py:50
  104.8 1.8 broadcast_in_dim.43
  106.5 1.9 broadcast_in_dim.43.clone
  109.6 139.5 %while.20 = (s32[]{:T(128)}, bf16[256,2560]{1,0:T(8,128)(2,1)}, bf16[256,2560]{1,0:T(8,128)(2,1)S(1)}, f32[256,2560]{1,0:T(8,128)}, f32[256,2560]{1,0:T(8,128)},...) while((s32[]{:T(128)}, bf16[256,2560]{1,0:T(8,128)(2,1)}, ...), condition=%wide.region_4.5_spmd.clone, body=%wide.region_0.4_spmd.clone.sunk | while | flops 169574656 | bytes 4862660 | solution.py:84
  109.7 1.3 fusion.70
  114.5 1.4 fusion.71
  116.6 1.3 fusion.70
  121.5 1.4 fusion.71
  123.6 1.3 fusion.70
  128.4 1.4 fusion.71
  135.4 1.4 fusion.71
  137.5 1.3 fusion.70
  142.3 1.4 fusion.71
  144.5 1.3 fusion.70
  149.4 1.4 fusion.71
  151.5 1.3 fusion.70
  156.3 1.4 fusion.71
  158.5 1.3 fusion.70
  163.3 1.4 fusion.71
  170.3 1.4 fusion.71
  172.4 1.3 fusion.70
  177.3 1.4 fusion.71
  179.4 1.3 fusion.70
  184.3 1.4 fusion.71
  191.2 1.4 fusion.71
  193.3 1.3 fusion.70
  198.2 1.4 fusion.71
  205.2 1.4 fusion.71
  212.1 1.4 fusion.71
  214.3 1.3 fusion.70
  219.1 1.4 fusion.71
  226.1 1.4 fusion.71
  228.2 1.3 fusion.70
  233.0 1.4 fusion.71
  240.1 1.4 fusion.71
  242.2 1.3 fusion.70
  247.0 1.4 fusion.71
  249.2 1.3 collective-permute-start.1
  250.5 4.7 %all-to-all-start.4 = ((bf16[2,128,2560]{2,1,0:T(8,128)(2,1)}), bf16[2,128,2560]{2,1,0:T(8,128)(2,1)}, u32[]{:S(2)}, u32[]{:S(2)}) async-start(bf16[2,128,2560]{2,1,0:T(8,128)(2,1)} %bitcast.72), calls=%async_computation.4 | async-start | bytes 2621440 | tf_op jit(solution)/shard_map/all_to_all | solution.py:91
  255.2 18.3 %all_gather.3 = bf16[256,128]{0,1:T(8,128)(2,1)S(1)} all-gather(bf16[128,128]{0,1:T(8,128)(2,1)S(1)} %pad_maximum_fusion.4), channel_id=1, replica_groups=mesh['blk'=16,'uly'=2] {'uly'}, dimensions={0}, use_global_device_ids=true | all-gather | bytes 98304 | tf_op jit(solution)/shard_map/all_gather | solution.py:92
  275.1 1.8 copy.35
  276.9 1.4 copy.36
  278.3 2.9 add_convert_fusion
  283.6 12.9 %reduce-scatter.2.cloned.1.call-done = f32[128,128]{0,1:T(8,128)} async-done(((f32[256,128]{0,1:T(8,128)}), f32[128,128]{0,1:T(8,128)}) %reduce-scatter.2.cloned.1.call-update) | async-done | bytes 65552 | tf_op jit(solution)/shard_map/reduce_scatter | solution.py:102
  296.4 2.8 convolution_bitcast_fusion
  299.3 74.1 %all-reduce.5 = bf16[5120,128]{0,1:T(8,128)(2,1)S(1)} all-reduce(f32[5120,128]{0,1:T(8,128)} %convolution_bitcast_fusion), channel_id=1, replica_groups=mesh['blk'=16,'uly'=2] {'blk','uly'}, use_global_device_ids=true, to_apply=%region_6.7 | all-reduce | flops 655360 | bytes 3932160 | tf_op jit(solution)/shard_map/psum | solution.py:105
  374.5 7.9 %all-reduce.4.cloned.1.call-done = (bf16[64,2560]{1,0:T(8,128)(2,1)}, bf16[64,2560]{1,0:T(8,128)(2,1)}) async-done(((bf16[64,2560]{1,0:T(8,128)(2,1)}, bf16[64,2560]{1,0:T(8,128)(2,1)}), (bf16[64,2560]{1,0:T(8,128)(2,1)}, bf16[64,2560]{1,0:T(8,128)(2,1)})) %all-reduce.4.cloned.1.call-update) | async-done | bytes 655376 | tf_op jit(solution)/shard_map/psum | solution.py:109
  382.4 1.7 copy.76
  384.1 1.7 copy.77
  (267 shorter events, 106.5 us)
Async XLA Ops:
  8.0 1.3 copy-start
  8.0 3.0 copy-start.7
  8.0 3.0 copy-start.5
  12.7 21.5 %all-to-all-start.2 = ((bf16[128,2,2560]{2,0,1:T(8,128)(2,1)}), bf16[128,2,2560]{2,0,1:T(8,128)(2,1)S(1)}, u32[]{:S(2)}, u32[]{:S(2)}) async-start(bf16[128,2,2560]{2,0,1:T(8,128)(2,1)} %bitcast.73), calls=%async_computation.2 | async-start | bytes 2621440 | tf_op jit(solution)/shard_map/all_to_all | solution.py:52
  53.9 1.9 copy-start.1
  55.8 34.6 %collective-permute-start = (bf16[2,256,2560]{2,1,0:T(8,128)(2,1)}, bf16[2,256,2560]{2,1,0:T(8,128)(2,1)}, u32[]{:S(2)}, u32[]{:S(2)}) collective-permute-start(bf16[2,256,2560]{2,1,0:T(8,128)(2,1)} %pad_maximum_fusion), channel_id=1, source_target_pairs={{0,2},{2,4},{4,6},{6,8},{8,10},{10,12},{12,14},{14,16},{16,18},{18... | collective-permute-start | bytes 7864328 | tf_op jit(solution)/shard_map/ppermute | solution.py:12
  61.1 4.7 %copy-start.9 = (bf16[5120,64]{0,1:T(8,128)(2,1)S(1)}, bf16[5120,64]{0,1:T(8,128)(2,1)}, u32[]{:S(2)}) copy-start(bf16[5120,64]{0,1:T(8,128)(2,1)} %param.16) | copy-start | bytes 1966084
  61.1 22.3 %all-to-all-start.3 = ((bf16[128,2,2560]{0,2,1:T(8,128)(2,1)}), bf16[128,2,2560]{0,2,1:T(8,128)(2,1)}, u32[]{:S(2)}, u32[]{:S(2)}) async-start(bf16[128,2,2560]{0,2,1:T(8,128)(2,1)} %bitcast.71), calls=%async_computation.3 | async-start | bytes 2621440 | tf_op jit(solution)/shard_map/all_to_all | solution.py:53
  65.8 1.1 copy-start.3
  65.8 1.5 copy-start.8
  83.4 21.3 %all-to-all-start = ((bf16[128,2,2560]{2,0,1:T(8,128)(2,1)}), bf16[128,2,2560]{2,0,1:T(8,128)(2,1)}, u32[]{:S(2)}, u32[]{:S(2)}) async-start(bf16[128,2,2560]{2,0,1:T(8,128)(2,1)} %bitcast.70), calls=%async_computation | async-start | bytes 2621440 | tf_op jit(solution)/shard_map/all_to_all | solution.py:50
  90.4 2.1 copy-start.2
  249.2 29.1 %collective-permute-start.1 = (f32[256,2560]{1,0:T(8,128)}, f32[256,2560]{1,0:T(8,128)}, u32[]{:S(2)}, u32[]{:S(2)}) collective-permute-start(f32[256,2560]{1,0:T(8,128)} %get-tuple-element.180), channel_id=1, source_target_pairs={{2,0},{4,2},{6,4},{8,6},{10,8},{12,10},{14,12},{16,14},{18,16},{20... | collective-permute-start | bytes 7864328 | tf_op jit(solution)/shard_map/ppermute | solution.py:12
  250.4 23.0 %copy-start.4 = (bf16[64,5120]{1,0:T(8,128)(2,1)S(1)}, bf16[64,5120]{1,0:T(8,128)(2,1)}, u32[]{:S(2)}) copy-start(bf16[64,5120]{1,0:T(8,128)(2,1)} %param.17) | copy-start | bytes 1966084
  250.5 24.6 %all-to-all-start.4 = ((bf16[2,128,2560]{2,1,0:T(8,128)(2,1)}), bf16[2,128,2560]{2,1,0:T(8,128)(2,1)}, u32[]{:S(2)}, u32[]{:S(2)}) async-start(bf16[2,128,2560]{2,1,0:T(8,128)(2,1)} %bitcast.72), calls=%async_computation.4 | async-start | bytes 2621440 | tf_op jit(solution)/shard_map/all_to_all | solution.py:91
  255.1 41.3 %reduce-scatter.2.cloned.1.call-start = ((), (), s32[]{:S(2)}) async-start(), calls=%async_computation.6 | async-start | bytes 196608 | tf_op jit(solution)/shard_map/reduce_scatter | solution.py:102
  278.3 2.9 copy-start.6
  282.4 99.9 %all-reduce.4.cloned.1.call-start = ((), (), s32[]{:S(2)}) async-start(), calls=%async_computation.7 | async-start | bytes 1310720 | tf_op jit(solution)/shard_map/psum | solution.py:109
Sparse Core Ops, SparseCore 0:
  282.5 13.8 reduce-scatter.1
Sparse Core Ops, SparseCore 1:
  286.9 95.4 all-reduce.3
where the time goes:
time: 396 us; the launch traced here: 393 us
  blocking collectives  112 us (28%)
  matrix products  89.7 us (23%)
  local copies, waits for them, and re-layouts  76.7 us (19%)
  waiting for transfers between devices  59.7 us (15%)
  starting transfers between devices  22.2 us (6%)
  other arithmetic  16.2 us (4%)
  between operations  15.7 us (4%)
    psum x1, blocking collectives, per_device(): down_total = lax.psum(inner(tokens, lowrank), ('blk', 'uly'))  74.1 us
    dot_general x20, matrix products, head_pass(): jnp.dot(score_grad, keys, preferred_element_type=jnp.float32) * scale  27.2 us
    dot_general x20, matrix products, head_pass(): scores = jnp.dot(query, keys.T, preferred_element_type=jnp.float32) * scale  25.1 us
    dot_general x20, matrix products, head_pass(): jnp.dot(probs, values, preferred_element_type=jnp.float32)  23.1 us
    all_to_all x1, blocking collectives, per_device(): lax.all_to_all(key_base, 'uly', split_axis=1, concat_axis=0, tiled=True)  19.7 us
    dynamic_slice x40, local copies, waits for them, and re-layouts, per_head(): lax.dynamic_slice_in_dim(upstream_h, start, HEAD, 1)  19.1 us
    all_gather x1, blocking collectives, per_device(): lax.all_gather(jnp.concatenate([low_q, low_v], 1), 'uly', axis=0, tiled=T...  18.3 us
    dynamic_update_slice x20, local copies, waits for them, and re-layouts, per_head(): lax.dynamic_update_slice_in_dim(prior_terms, result[2][:rows], start, 1)  15.6 us
  transfers between devices with their start and end apart: 8, of which 5 were waited for; matrix products, arithmetic and copies ran while one was open for 6% of the time, Pallas kernels for 0%

commit v1 on v0

--- a/solution.py
+++ b/solution.py
@@ -102,7 +102,7 @@
     lowrank = lax.psum_scatter(partial_rank, "uly", scatter_dimension=0, tiled=True).astype(
         jnp.bfloat16
     )
-    down_total = lax.psum(inner(tokens, lowrank), ("blk", "uly"))
+    down_total = lax.psum(lax.psum(inner(tokens, lowrank), "uly"), "blk")
     up_q_terms = inner(block_lows[:, :rank], query_grad_h)
     up_v_terms = inner(block_lows[:, rank:], value_grad_h)
     up_q_part, up_v_part = (

time: 396 us -> 501 us (1.27)
  waiting for transfers between devices: 59.7 us -> 145 us
  blocking collectives: 112 us -> 129 us
    psum x0 -> x1, waiting for transfers between devices: none -> 44.8 us  [per_device(): down_total = lax.psum(lax.psum(inner(tokens, lowrank), 'uly'), 'blk')]
    reduce_scatter x1, waiting for transfers between devices: 12.9 us -> 36 us  [per_device(): lax.psum_scatter(partial_rank, 'uly', scatter_dimension=0, tiled=True)]
    all_gather x1, blocking collectives: 18.3 us -> 32.1 us  [per_device(): lax.all_gather(jnp.concatenate([low_q, low_v], 1), 'uly', axis=0, tiled=T...]
    psum x1, waiting for transfers between devices: 7.86 us -> 21.1 us  [per_device(): lax.psum(up_q_terms.astype(jnp.bfloat16), 'blk').astype(jnp.float32)]
    unnamed x24 -> x26, local copies, waits for them, and re-layouts: 9.74 us -> 11.9 us
  transfers between devices with their start and end apart: 8 -> 9, of which waited for: 5 -> 7; matrix products, arithmetic and copies ran while one was open for 6% -> 5% of each run, Pallas kernels for 0% -> 0%
where the time goes in v1:
time: 501 us; the launch traced here: 498 us
  waiting for transfers between devices  145 us (29%)
  blocking collectives  129 us (26%)
  matrix products  90.7 us (18%)
  local copies, waits for them, and re-layouts  79.7 us (16%)
  starting transfers between devices  22.1 us (4%)
  other arithmetic  16.2 us (3%)
  between operations  13.9 us (3%)
    psum x1, blocking collectives, per_device(): down_total = lax.psum(lax.psum(inner(tokens, lowrank), 'uly'), 'blk')  77.1 us
    psum x1, waiting for transfers between devices, per_device(): down_total = lax.psum(lax.psum(inner(tokens, lowrank), 'uly'), 'blk')  44.8 us
    reduce_scatter x1, waiting for transfers between devices, per_device(): lax.psum_scatter(partial_rank, 'uly', scatter_dimension=0, tiled=True)  36 us
    all_gather x1, blocking collectives, per_device(): lax.all_gather(jnp.concatenate([low_q, low_v], 1), 'uly', axis=0, tiled=T...  32.1 us
    dot_general x20, matrix products, head_pass(): jnp.dot(score_grad, keys, preferred_element_type=jnp.float32) * scale  27.2 us
    dot_general x20, matrix products, head_pass(): scores = jnp.dot(query, keys.T, preferred_element_type=jnp.float32) * scale  25.1 us
    dot_general x20, matrix products, head_pass(): jnp.dot(probs, values, preferred_element_type=jnp.float32)  23.1 us
    psum x1, waiting for transfers between devices, per_device(): lax.psum(up_q_terms.astype(jnp.bfloat16), 'blk').astype(jnp.float32)  21.1 us
  transfers between devices with their start and end apart: 9, of which 7 were waited for; matrix products, arithmetic and copies ran while one was open for 5% of the time, Pallas kernels for 0%

profile of v1, /device:TPU:0, one launch (start us, length us, event | category | flops | bytes accessed | tf_op | source)
XLA Modules:
  0.0 497.6 jit_solution(5049458562276672925)
XLA Ops:
  7.2 1.3 copy-done
  8.5 1.7 convolution_convert_fusion.3
  11.9 4.2 all-to-all-start.2
  16.1 2.5 copy.47
  18.6 14.8 %all-to-all-done.2 = bf16[128,2,2560]{2,0,1:T(8,128)(2,1)S(1)} async-done(((bf16[128,2,2560]{2,0,1:T(8,128)(2,1)}), bf16[128,2,2560]{2,0,1:T(8,128)(2,1)S(1)}, u32[]{:S(2)}, u32[]{:S(2)}) %all-to-all-start.2) | async-done | bytes 1310752 | tf_op jit(solution)/shard_map/all_to_all | solution.py:52
  33.4 19.7 %all_to_all.95 = bf16[128,2,2560]{2,0,1:T(8,128)(2,1)S(1)} all-to-all(bf16[128,2,2560]{2,0,1:T(8,128)(2,1)} %bitcast.74), channel_id=1, replica_groups=mesh['blk'=16,'uly'=2] {'uly'}, dimensions={1} | all-to-all | bytes 2621440 | tf_op jit(solution)/shard_map/all_to_all | solution.py:51
  53.1 1.9 pad_maximum_fusion
  55.0 2.8 collective-permute-start
  57.9 2.5 copy.30
  60.4 4.6 all-to-all-start.3
  68.2 14.4 %all-to-all-done.3 = bf16[128,2,2560]{0,2,1:T(8,128)(2,1)} async-done(((bf16[128,2,2560]{0,2,1:T(8,128)(2,1)}), bf16[128,2,2560]{0,2,1:T(8,128)(2,1)}, u32[]{:S(2)}, u32[]{:S(2)}) %all-to-all-start.3) | async-done | bytes 1310752 | tf_op jit(solution)/shard_map/all_to_all | solution.py:53
  82.6 4.5 all-to-all-start
  87.2 2.5 copy.31
  89.7 2.0 slice_bitcast_fusion
  91.8 2.5 pad_maximum_fusion.1
  94.3 9.6 %all-to-all-done = bf16[128,2,2560]{2,0,1:T(8,128)(2,1)} async-done(((bf16[128,2,2560]{2,0,1:T(8,128)(2,1)}), bf16[128,2,2560]{2,0,1:T(8,128)(2,1)}, u32[]{:S(2)}, u32[]{:S(2)}) %all-to-all-start) | async-done | bytes 1310752 | tf_op jit(solution)/shard_map/all_to_all | solution.py:50
  103.9 1.8 broadcast_in_dim.43
  105.7 1.9 broadcast_in_dim.43.clone
  108.8 139.5 %while.20 = (s32[]{:T(128)}, bf16[256,2560]{1,0:T(8,128)(2,1)}, bf16[256,2560]{1,0:T(8,128)(2,1)S(1)}, f32[256,2560]{1,0:T(8,128)}, f32[256,2560]{1,0:T(8,128)},...) while((s32[]{:T(128)}, bf16[256,2560]{1,0:T(8,128)(2,1)}, ...), condition=%wide.region_4.5_spmd.clone, body=%wide.region_0.4_spmd.clone.sunk | while | flops 169574656 | bytes 4862660 | solution.py:84
  108.8 1.3 fusion.70
  113.7 1.4 fusion.71
  115.8 1.3 fusion.70
  120.7 1.4 fusion.71
  127.7 1.4 fusion.71
  134.7 1.4 fusion.71
  141.7 1.4 fusion.71
  143.8 1.3 fusion.70
  148.6 1.4 fusion.71
  150.8 1.3 fusion.70
  155.6 1.4 fusion.71
  157.7 1.3 fusion.70
  162.6 1.4 fusion.71
  164.7 1.3 fusion.70
  169.5 1.4 fusion.71
  176.5 1.4 fusion.71
  183.5 1.4 fusion.71
  190.5 1.4 fusion.71
  192.6 1.3 fusion.70
  197.4 1.4 fusion.71
  204.4 1.4 fusion.71
  211.4 1.4 fusion.71
  213.6 1.3 fusion.70
  218.4 1.4 fusion.71
  225.3 1.4 fusion.71
  232.3 1.4 fusion.71
  234.4 1.3 fusion.70
  239.3 1.4 fusion.71
  241.4 1.3 fusion.70
  246.2 1.4 fusion.71
  248.3 1.3 collective-permute-start.1
  249.6 1.5 fusion.26
  251.1 4.3 collective-permute-done.1
  255.5 2.9 add_convert_fusion
  260.7 36.0 %reduce-scatter.2.cloned.1.call-done = f32[128,128]{0,1:T(8,128)} async-done(((f32[256,128]{0,1:T(8,128)}), f32[128,128]{0,1:T(8,128)}) %reduce-scatter.2.cloned.1.call-update) | async-done | bytes 65552 | tf_op jit(solution)/shard_map/reduce_scatter | solution.py:102
  296.8 2.8 convolution_bitcast_fusion
  299.6 4.5 all-to-all-start.4
  304.2 32.1 %all_gather.3 = bf16[256,128]{0,1:T(8,128)(2,1)S(1)} all-gather(bf16[128,128]{0,1:T(8,128)(2,1)S(1)} %pad_maximum_fusion.4), channel_id=1, replica_groups=mesh['blk'=16,'uly'=2] {'uly'}, dimensions={0}, use_global_device_ids=true | all-gather | bytes 98304 | tf_op jit(solution)/shard_map/all_gather | solution.py:92
  337.4 2.5 copy.35
  340.0 2.5 copy.36
  343.6 44.8 %all-reduce.5.cloned.1.call-done = f32[5120,128]{0,1:T(8,128)} async-done(((f32[5120,128]{0,1:T(8,128)}), f32[5120,128]{0,1:T(8,128)}) %all-reduce.5.cloned.1.call-update) | async-done | bytes 2621456 | tf_op jit(solution)/shard_map/psum | solution.py:105
  388.3 77.1 %all-reduce.8 = bf16[5120,128]{0,1:T(8,128)(2,1)S(1)} all-reduce(f32[5120,128]{0,1:T(8,128)} %all-reduce.5.cloned.1.call-done), channel_id=1, replica_groups=mesh['blk'=16,'uly'=2] {'blk'}, use_global_device_ids=true, to_apply=%region_7.8 | all-reduce | flops 655360 | bytes 3932160 | tf_op jit(solution)/shard_map/psum | solution.py:105
  466.6 21.1 %all-reduce.7.cloned.1.call-done = (bf16[64,2560]{1,0:T(8,128)(2,1)}, bf16[64,2560]{1,0:T(8,128)(2,1)}) async-done(((bf16[64,2560]{1,0:T(8,128)(2,1)}, bf16[64,2560]{1,0:T(8,128)(2,1)}), (bf16[64,2560]{1,0:T(8,128)(2,1)}, bf16[64,2560]{1,0:T(8,128)(2,1)})) %all-reduce.7.cloned.1.call-update) | async-done | bytes 655376 | tf_op jit(solution)/shard_map/psum | solution.py:109
  487.7 1.7 copy.77
  489.4 1.7 copy.78
  (272 shorter events, 110.9 us)
Async XLA Ops:
  7.2 1.3 copy-start
  7.2 3.0 copy-start.8
  7.2 3.0 copy-start.6
  11.9 21.5 %all-to-all-start.2 = ((bf16[128,2,2560]{2,0,1:T(8,128)(2,1)}), bf16[128,2,2560]{2,0,1:T(8,128)(2,1)S(1)}, u32[]{:S(2)}, u32[]{:S(2)}) async-start(bf16[128,2,2560]{2,0,1:T(8,128)(2,1)} %bitcast.73), calls=%async_computation.2 | async-start | bytes 2621440 | tf_op jit(solution)/shard_map/all_to_all | solution.py:52
  53.1 1.9 copy-start.1
  55.0 34.6 %collective-permute-start = (bf16[2,256,2560]{2,1,0:T(8,128)(2,1)}, bf16[2,256,2560]{2,1,0:T(8,128)(2,1)}, u32[]{:S(2)}, u32[]{:S(2)}) collective-permute-start(bf16[2,256,2560]{2,1,0:T(8,128)(2,1)} %pad_maximum_fusion), channel_id=1, source_target_pairs={{0,2},{2,4},{4,6},{6,8},{8,10},{10,12},{12,14},{14,16},{16,18},{18... | collective-permute-start | bytes 7864328 | tf_op jit(solution)/shard_map/ppermute | solution.py:12
  60.4 4.7 copy-start.10
  60.4 22.3 %all-to-all-start.3 = ((bf16[128,2,2560]{0,2,1:T(8,128)(2,1)}), bf16[128,2,2560]{0,2,1:T(8,128)(2,1)}, u32[]{:S(2)}, u32[]{:S(2)}) async-start(bf16[128,2,2560]{0,2,1:T(8,128)(2,1)} %bitcast.71), calls=%async_computation.3 | async-start | bytes 2621440 | tf_op jit(solution)/shard_map/all_to_all | solution.py:53
  65.0 1.1 copy-start.5
  65.0 1.5 copy-start.9
  82.6 21.3 %all-to-all-start = ((bf16[128,2,2560]{2,0,1:T(8,128)(2,1)}), bf16[128,2,2560]{2,0,1:T(8,128)(2,1)}, u32[]{:S(2)}, u32[]{:S(2)}) async-start(bf16[128,2,2560]{2,0,1:T(8,128)(2,1)} %bitcast.70), calls=%async_computation | async-start | bytes 2621440 | tf_op jit(solution)/shard_map/all_to_all | solution.py:50
  87.2 209.6 %reduce-scatter.2.cloned.1.call-start = ((), (), s32[]{:S(2)}) async-start(), calls=%async_computation.6 | async-start | bytes 196608 | tf_op jit(solution)/shard_map/reduce_scatter | solution.py:102
  89.7 2.1 copy-start.2
  248.3 7.1 %collective-permute-start.1 = (f32[256,2560]{1,0:T(8,128)}, f32[256,2560]{1,0:T(8,128)}, u32[]{:S(2)}, u32[]{:S(2)}) collective-permute-start(f32[256,2560]{1,0:T(8,128)} %get-tuple-element.180), channel_id=1, source_target_pairs={{2,0},{4,2},{6,4},{8,6},{10,8},{12,10},{14,12},{16,14},{18,16},{20... | collective-permute-start | bytes 7864328 | tf_op jit(solution)/shard_map/ppermute | solution.py:12
  255.5 4.0 copy-start.7
  258.4 1.1 copy-start.3
  260.7 127.7 %all-reduce.5.cloned.1.call-start = ((), (), s32[]{:S(2)}) async-start(), calls=%async_computation.7 | async-start | bytes 5242880 | tf_op jit(solution)/shard_map/psum | solution.py:105
  299.6 37.8 %all-to-all-start.4 = ((bf16[2,128,2560]{2,1,0:T(8,128)(2,1)}), bf16[2,128,2560]{2,1,0:T(8,128)(2,1)}, u32[]{:S(2)}, u32[]{:S(2)}) async-start(bf16[2,128,2560]{2,1,0:T(8,128)(2,1)} %bitcast.72), calls=%async_computation.4 | async-start | bytes 2621440 | tf_op jit(solution)/shard_map/all_to_all | solution.py:91
  304.2 183.5 %all-reduce.7.cloned.1.call-start = ((), (), s32[]{:S(2)}) async-start(), calls=%async_computation.8 | async-start | bytes 1310720 | tf_op jit(solution)/shard_map/psum | solution.py:109
  340.0 2.5 copy-start.4
Sparse Core Ops, SparseCore 0:
  260.8 35.9 reduce-scatter.1
  299.7 88.5 all-reduce.4
  392.4 95.2 all-reduce.6
